TPU v7x, 256 devices: a whole 4x4x8 slice. The times are simulated.
256 devices in a mesh: row: 8 (over y, x_lo), col: 32 (over z, x_hi, core).
Axes of the slice: x: 4 (x_hi: 2, x_lo: 2; x = x_hi * 2 + x_lo), y: 4, z: 8, core: 2. Of those that a mesh axis runs over, the one named last changes fastest.
Arguments:
- grad_out: bfloat16 [3072, 8192], P('row', 'col'), may hold values from -6 to 6
- gate_act: bfloat16 [3072, 28672], P('row', 'col'), may hold values from -6 to 6
- up_act: bfloat16 [3072, 28672], P('row', 'col'), may hold values from -6 to 6
- down_weight: bfloat16 [28672, 8192], P('col', 'row'), may hold values from -0.0625 to 0.0625
Outputs:
- grad_gate: bfloat16 [3072, 28672], P('row', 'col')
- grad_up: bfloat16 [3072, 28672], P('row', 'col')
- grad_weight: float32 [28672, 8192], P('col', 'row')
All inputs are finite; a program needn't handle non-finite values.
Results may differ from a plain program's by a relative error of at most 0.0028.
Values may be sent and summed in bfloat16 or wider, within the bound.
A program may use at most 128 MiB of HBM per device.

v0:
```python
import jax
import jax.numpy as jnp
from jax import lax
from jax.sharding import PartitionSpec as P


def collect_features(grad_out):
    return lax.all_gather(grad_out, "col", axis=1, tiled=True)


def on_device(grad_out, gate_act, up_act, down_weight):
    token_major = lax.all_to_all(
        collect_features(grad_out), "row", split_axis=1, concat_axis=0, tiled=True
    )
    grad_rows = collect_features(grad_out)
    grad_hidden = lax.dot_general(
        grad_rows,
        lax.all_gather(down_weight, "row", axis=1, tiled=True),
        (((1,), (1,)), ((), ())),
        preferred_element_type=jnp.float32,
    )
    gate_value = gate_act.astype(jnp.float32)
    up_value = up_act.astype(jnp.float32)
    sigmoid_gate = jax.nn.sigmoid(gate_value)
    swish = gate_value * sigmoid_gate
    grad_gate = (
        grad_hidden * up_value * sigmoid_gate * (1.0 + gate_value * (1.0 - sigmoid_gate))
    ).astype(jnp.bfloat16)
    grad_up = (grad_hidden * swish).astype(jnp.bfloat16)
    hidden = (swish * up_value).astype(jnp.bfloat16)
    grad_weight = lax.dot_general(
        lax.all_gather(hidden, "row", axis=0, tiled=True),
        token_major,
        (((0,), (0,)), ((), ())),
        preferred_element_type=jnp.float32,
    )
    return (grad_gate, grad_up, grad_weight)


def solution(mesh):
    placed = (P("row", "col"), P("row", "col"), P("row", "col"), P("col", "row"))
    return jax.shard_map(
        on_device,
        mesh=mesh,
        in_specs=placed,
        out_specs=(P("row", "col"), P("row", "col"), P("col", "row")),
        check_vma=False,
    )
```

profile of v0, /device:TPU:3, one launch (start us, length us, event | category | flops | bytes accessed | tf_op | source)
XLA Modules:
  0.0 605.6 jit_solution(11016101793268797252)
XLA Ops:
  7.2 0.0 all-gather.4.cloned.1.call-start
  7.2 1.7 copy.7
  9.0 0.0 all-gather.4.cloned.1.call-update
  9.0 0.0 all-gather.6.cloned.1.call-start
  9.0 0.7 all-gather.6.cloned.1.call-update
  9.7 0.0 all-gather.8.cloned.1.call-start
  9.8 97.7 %all-gather.4.cloned.1.call-done = bf16[384,8192]{0,1:T(8,128)(2,1)} async-done(((bf16[384,256]{0,1:T(8,128)(2,1)}), bf16[384,8192]{0,1:T(8,128)(2,1)}) %all-gather.4.cloned.1.call-update) | async-done | bytes 6291472 | tf_op jit(solution)/shard_map/all_gather | solution.py:8
  107.5 287.8 %all-gather.6.cloned.1.call-done = bf16[896,8192]{1,0:T(8,128)(2,1)} async-done(((bf16[896,1024]{1,0:T(8,128)(2,1)}), bf16[896,8192]{1,0:T(8,128)(2,1)}) %all-gather.6.cloned.1.call-update) | async-done | bytes 14680080 | tf_op jit(solution)/shard_map/all_gather | solution.py:18
  395.3 13.8 %multiply_convert_fusion = (bf16[384,896]{1,0:T(8,128)(2,1)}, bf16[384,896]{1,0:T(8,128)(2,1)}, bf16[384,896]{1,0:T(8,128)(2,1)}) fusion(bf16[384,896]{1,0:T(8,128)(2,1)} %param.5, bf16[384,896]{1,0:T(8,128)(2,1)} %param.6, bf16[384,8192]{0,1:T(8,128)(2,1)} %all-gather.4.cloned.1.call-done, bf16[896,8192]{1,0:T(8,128)(2,1)} %all-gather.6.cloned.1.call-done), kind=kOutput, calls=%fused_computation.13 | convolution fusion | flops 5642993664 | bytes 24412160 | tf_op jit(solution)/shard_map/dot_general | solution.py:16
  409.1 0.0 all-gather.8.cloned.1.call-update
  409.1 134.1 %all_to_all.19 = bf16[384,8,1024]{0,2,1:T(8,128)(2,1)} all-to-all(bf16[384,8,1024]{0,2,1:T(8,128)(2,1)} %bitcast.8), channel_id=1, replica_groups=mesh['row'=8,'col'=32] {'row'}, dimensions={1} | all-to-all | bytes 12582912 | tf_op jit(solution)/shard_map/all_to_all | solution.py:12
  543.2 8.6 %copy.8 = bf16[8,384,1024]{2,1,0:T(8,128)(2,1)} copy(bf16[8,384,1024]{1,2,0:T(8,128)(2,1)} %bitcast.7) | data formatting | bytes 12582912 | tf_op jit(solution)/shard_map/all_to_all | solution.py:12
  551.8 36.5 %all-gather.8.cloned.1.call-done = bf16[3072,896]{1,0:T(8,128)(2,1)} async-done(((bf16[384,896]{1,0:T(8,128)(2,1)}), bf16[3072,896]{1,0:T(8,128)(2,1)}) %all-gather.8.cloned.1.call-update) | async-done | bytes 5505040 | tf_op jit(solution)/shard_map/all_gather | solution.py:32
  588.3 10.8 %fusion.8 = f32[896,1024]{1,0:T(8,128)} fusion(bf16[3072,896]{1,0:T(8,128)(2,1)} %all-gather.8.cloned.1.call-done, bf16[3072,1024]{1,0:T(8,128)(2,1)} %bitcast.9), kind=kOutput, calls=%fused_computation.14 | convolution fusion | flops 5637144576 | bytes 15466496 | tf_op jit(solution)/shard_map/dot_general | solution.py:31
Async XLA Ops:
  7.2 100.3 %all-gather.4.cloned.1.call-start = ((), (), s32[]{:S(2)}) async-start(), calls=%async_computation.1 | async-start | bytes 6488064 | tf_op jit(solution)/shard_map/all_gather | solution.py:8
  9.0 386.3 %all-gather.6.cloned.1.call-start = ((), (), s32[]{:S(2)}) async-start(), calls=%async_computation.2 | async-start | bytes 16515072 | tf_op jit(solution)/shard_map/all_gather | solution.py:18
  9.7 578.6 %all-gather.8.cloned.1.call-start = ((), (), s32[]{:S(2)}) async-start(), calls=%async_computation.3 | async-start | bytes 6193152 | tf_op jit(solution)/shard_map/all_gather | solution.py:32
Sparse Core Ops, SparseCore 0:
  11.3 96.1 all-gather.3
  109.3 285.9 all-gather.5
  409.2 178.9 all-gather.7
where the time goes:
time: 607 us; the launch traced here: 606 us
  waiting for transfers between devices  423 us (70%)
  blocking collectives  134 us (22%)
  matrix products  24.7 us (4%)
  between operations  13.7 us (2%)
  local copies, waits for them, and re-layouts  10.4 us (2%)
    all_gather x1, waiting for transfers between devices, on_device(): lax.all_gather(down_weight, 'row', axis=1, tiled=True)  288 us
    all_to_all x1, blocking collectives, on_device(): lax.all_to_all(collect_features(grad_out), 'row', split_axis=1, concat_ax...  134 us
    all_gather x1, waiting for transfers between devices, collect_features(): return lax.all_gather(grad_out, 'col', axis=1, tiled=True)  97.7 us
    all_gather x1, waiting for transfers between devices, on_device(): lax.all_gather(hidden, 'row', axis=0, tiled=True)  36.5 us
    dot_general x1, matrix products, on_device(): lax.dot_general(grad_rows, lax.all_gather(down_weight, 'row', axis=1, til...  13.8 us
  transfers between devices with their start and end apart: 3, of which 3 were waited for; matrix products, arithmetic and copies ran while one was open for 1% of the time, Pallas kernels for 0%

commit v1 on v0

v1 whole, which is shorter than its diff:
```python
import jax
import jax.numpy as jnp
from jax import lax
from jax.experimental import pallas as pl
from jax.experimental.pallas import tpu as pltpu
from jax.sharding import PartitionSpec as P

MESH = pl.DeviceIdType.MESH
TB = 384
FB = 896
DR = 1024
DC = 256
CH = 4
NQ = 4 * CH
ROWS = TB // CH
HOPS = 7
SKEW = 2
F_TILES = ((0, 256), (256, 256), (512, 256), (768, 128))


def place(j):
    return j + lax.div(j, 2) - 2 * lax.div(j, 3)


ORDER = (0, 1, 3, 2)


def kernel(
    g_hbm, ga_hbm, up_hbm, w_hbm, gg_hbm, gu_hbm, gw_hbm,
    g1, g2, w2, ht, part, got, acc, ga, up, ggv, guv, gwv,
    loc_sem, out_sem,
    send_a, recv_a, send_w, recv_w, send_h, recv_h, send_r, recv_r,
    send_z, recv_z, send_s, recv_s, send_o, recv_o, send_p, recv_p,
):
    r = lax.axis_index("row")
    c = lax.axis_index("col")
    y, xl = lax.div(r, 2), lax.rem(r, 2)
    z = lax.div(c, 4)
    xh = lax.rem(lax.div(c, 2), 2)
    k = lax.rem(c, 2)
    sib = (r, c + 1 - 2 * k)
    partner = (r + 1 - 2 * xl, c)
    outer = (r + 1 - 2 * xl, c + 2 - 4 * xh)
    c2 = c + 2 - 4 * xh

    def ring_y(o):
        return lax.rem(r + 2 * o, 8)

    z_next = (
        (r, lax.rem(c + 4, 32)),
        (r, lax.rem(c + 28, 32)),
    )

    def remote(src, dst, ssem, rsem, dev):
        return pltpu.make_async_remote_copy(
            src_ref=src, dst_ref=dst, send_sem=ssem, recv_sem=rsem,
            device_id=dev, device_id_type=MESH,
        )

    def arrived(ref, sem):
        pltpu.make_async_copy(ref, ref, sem).wait()

    load_ga = pltpu.make_async_copy(ga_hbm, ga, loc_sem.at[0])
    load_up = pltpu.make_async_copy(up_hbm, up, loc_sem.at[1])
    load_w = pltpu.make_async_copy(w_hbm, w2.at[xl], loc_sem.at[2])
    load_ga.start()
    load_up.start()
    load_w.start()

    barrier = pltpu.get_barrier_semaphore()
    peers = [(ring_y(o), c) for o in (1, 2, 3)]
    peers += [(ring_y(o), c2) for o in (0, 1, 2, 3)]
    peers += [sib, partner, outer, z_next[0], z_next[1]]
    for dev in peers:
        pl.semaphore_signal(barrier, inc=1, device_id=dev, device_id_type=MESH)

    load_ga.wait()
    load_up.wait()

    def hidden_tile(i, carry):
        cols = pl.ds(pl.multiple_of(i * 128, 128), 128)
        gv = ga[:, cols].astype(jnp.float32)
        uv = up[:, cols].astype(jnp.float32)
        hv = gv * jax.nn.sigmoid(gv) * uv
        ht[r, cols, :] = hv.T.astype(jnp.bfloat16)
        return carry

    lax.fori_loop(0, FB // 128, hidden_tile, 0)

    pl.semaphore_wait(barrier, len(peers))

    yr = lax.div(z, 2)
    zb_own = lax.rem(z, 2)
    unit_cols = pl.ds(pl.multiple_of((2 * xh + k) * DC, DC), DC)
    a_dst = g1.at[zb_own, y, :, unit_cols]
    root_row = 2 * yr + xl
    a_slot = y * 2 + xh
    a_far = remote(g_hbm, a_dst, send_a.at[1], recv_a.at[a_slot], (root_row, c2))
    a_near = remote(g_hbm, a_dst, send_a.at[0], recv_a.at[a_slot], (root_row, c))
    a_local = pltpu.make_async_copy(g_hbm, a_dst, recv_a.at[a_slot])

    @pl.when(yr == y)
    def _():
        a_local.start()

    @pl.when(yr != y)
    def _():
        a_near.start()

    a_far.start()

    def hidden_sends(slot, base, devs):
        out = []
        for i, dev in enumerate(devs):
            out.append(
                remote(ht.at[slot], ht.at[slot], send_h.at[base + i], recv_h.at[slot], dev)
            )
        return out

    y_devs = [(ring_y(o), c) for o in (1, 3, 2)]
    own_h = hidden_sends(r, 0, y_devs + [partner])
    for d in own_h[:3]:
        d.start()

    w_sends = []
    for i, (f0, fn) in enumerate(F_TILES):
        w_sends.append(
            remote(
                w_hbm.at[pl.ds(f0, fn), :], w2.at[xl, pl.ds(f0, fn), :],
                send_w.at[i], recv_w.at[i], partner,
            )
        )
    w_sends[0].start()
    own_h[3].start()
    for d in w_sends[1:]:
        d.start()

    def lane_distance(zb, way):
        root = 2 * y + zb
        if way == 0:
            return lax.rem(z - root + 8, 8)
        return lax.rem(root - z + 8, 8)

    def lane_cols(way):
        return pl.ds(pl.multiple_of((2 * way + k) * DC, DC), DC)

    def block_of(j):
        return lax.rem(y + place(j), 4)

    def z_step(s, carry):
        for zb in range(2):
            for way in range(2):
                lane = 2 * zb + way
                d = lane_distance(zb, way)
                q = s - d

                @pl.when(jnp.logical_and(q >= 0, q < NQ))
                def _(zb=zb, way=way, lane=lane, d=d, q=q):
                    j = lax.div(q, CH)
                    p = lax.rem(q, CH)
                    yb = block_of(j)
                    rows = pl.ds(pl.multiple_of(p * ROWS, ROWS), ROWS)
                    ref = g1.at[zb, yb, rows, lane_cols(way)]

                    @pl.when(jnp.logical_and(d == 0, p == 0))
                    def _():
                        arrived(g1.at[zb, yb, :, lane_cols(way)], recv_a.at[yb * 2 + way])

                    @pl.when(d != 0)
                    def _():
                        arrived(ref, recv_z.at[lane * NQ + q])

                    @pl.when(d < HOPS)
                    def _():
                        remote(
                            ref, ref, send_z.at[lane], recv_z.at[lane * NQ + q], z_next[way]
                        ).start()

                    remote(ref, ref, send_s.at[lane], recv_s.at[lane * 4 + j], sib).start()

                    @pl.when(xl == 1 - zb)
                    def _():
                        remote(
                            ref, g2.at[yb, rows, lane_cols(way)],
                            send_o.at[way], recv_o.at[way * NQ + q], outer,
                        ).start()

        for way in range(2):
            d = jnp.where(xl == 0, lane_distance(0, way), lane_distance(1, way))
            q = s - SKEW - d

            @pl.when(jnp.logical_and(q >= 0, q < NQ))
            def _(way=way, q=q):
                j = lax.div(q, CH)
                p = lax.rem(q, CH)
                yb = block_of(j)
                rows = pl.ds(pl.multiple_of(p * ROWS, ROWS), ROWS)
                ref = g2.at[yb, rows, lane_cols(way)]
                arrived(ref, recv_o.at[way * NQ + q])
                remote(ref, ref, send_p.at[way], recv_p.at[way * 4 + j], sib).start()

        return carry

    half = NQ // 2
    last = NQ + HOPS + SKEW
    lax.fori_loop(0, half, z_step, 0)

    slot_p = r + 1 - 2 * xl
    arrived(ht.at[slot_p], recv_h.at[slot_p])
    fwd_h = hidden_sends(slot_p, 4, y_devs)
    for d in fwd_h:
        d.start()

    lax.fori_loop(half, last, z_step, 0)

    load_w.wait()
    for i, (f0, fn) in enumerate(F_TILES):
        arrived(w2.at[1 - xl, pl.ds(f0, fn), :], recv_w.at[i])

    nt = (((1,), (1,)), ((), ()))

    def product(yb, f0, fn):
        total = None
        for zb in range(2):
            term = lax.dot_general(
                g1[zb, yb], w2[zb, pl.ds(f0, fn), :], nt, preferred_element_type=jnp.float32
            )
            total = term if total is None else total + term
        return total

    r_sends = []
    for j in range(1, 4):
        o = ORDER[j]
        yb = lax.rem(y + o, 4)
        for zb in range(2):
            for way in range(2):
                lane = 2 * zb + way
                cols = pl.ds(pl.multiple_of((2 * way + 1 - k) * DC, DC), DC)
                arrived(g1.at[zb, yb, :, cols], recv_s.at[lane * 4 + j])
        for f0, fn in F_TILES:
            part[o - 1, :, f0 : f0 + fn] = product(yb, f0, fn).astype(jnp.bfloat16)
        send = remote(
            part.at[o - 1], got.at[o - 1], send_r.at[o - 1], recv_r.at[o - 1], (ring_y(o), c)
        )
        send.start()
        r_sends.append(send)

    for zb in range(2):
        for way in range(2):
            lane = 2 * zb + way
            cols = pl.ds(pl.multiple_of((2 * way + 1 - k) * DC, DC), DC)
            arrived(g1.at[zb, y, :, cols], recv_s.at[lane * 4])
    for f0, fn in F_TILES:
        acc[:, f0 : f0 + fn] = product(y, f0, fn)

    for way in range(2):
        cols = pl.ds(pl.multiple_of((2 * way + 1 - k) * DC, DC), DC)
        for j in range(4):
            yb = lax.rem(y + ORDER[j], 4)
            arrived(g2.at[yb, :, cols], recv_p.at[way * 4 + j])
    for o in (1, 3, 2):
        slot = ring_y(o)
        arrived(ht.at[slot], recv_h.at[slot])
    for o in (1, 3, 2):
        slot = lax.rem(slot_p + 2 * o, 8)
        arrived(ht.at[slot], recv_h.at[slot])

    def weight_tile(i, carry):
        cols = pl.ds(pl.multiple_of(i * 256, 256), 256)
        total = None
        for yb in range(4):
            for src, slot in ((g1.at[xl], 2 * yb + xl), (g2, 2 * yb + 1 - xl)):
                term = jnp.dot(
                    ht[slot], src[yb, :, cols], preferred_element_type=jnp.float32
                )
                total = term if total is None else total + term
        gwv[:, cols] = total
        pltpu.make_async_copy(gwv.at[:, cols], gw_hbm.at[:, cols], out_sem.at[2]).start()
        return carry

    lax.fori_loop(0, DR // 256, weight_tile, 0)

    for i in range(3):
        arrived(got.at[i], recv_r.at[i])

    def final_tile(i, carry):
        rows = pl.ds(pl.multiple_of(i * 32, 32), 32)
        gv = ga[rows, :].astype(jnp.float32)
        uv = up[rows, :].astype(jnp.float32)
        gh = acc[rows, :]
        for n in range(3):
            gh = gh + got[n, rows, :].astype(jnp.float32)
        s = jax.nn.sigmoid(gv)
        ggv[rows, :] = (gh * uv * s * (1.0 + gv * (1.0 - s))).astype(jnp.bfloat16)
        guv[rows, :] = (gh * (gv * s)).astype(jnp.bfloat16)
        return carry

    lax.fori_loop(0, TB // 32, final_tile, 0)
    out_gg = pltpu.make_async_copy(ggv, gg_hbm, out_sem.at[0])
    out_gu = pltpu.make_async_copy(guv, gu_hbm, out_sem.at[1])
    out_gg.start()
    out_gu.start()

    @pl.when(yr != y)
    def _():
        a_near.wait_send()

    a_far.wait_send()
    for d in own_h + fwd_h + w_sends + r_sends:
        d.wait_send()
    for zb in range(2):
        for way in range(2):
            lane = 2 * zb + way
            whole = g1.at[zb, :, :, lane_cols(way)]

            @pl.when(lane_distance(zb, way) < HOPS)
            def _(whole=whole, lane=lane):
                arrived(whole, send_z.at[lane])

            arrived(whole, send_s.at[lane])
    for way in range(2):
        whole = g2.at[:, :, lane_cols(way)]
        arrived(whole, send_o.at[way])
        arrived(whole, send_p.at[way])
    pltpu.make_async_copy(gwv, gw_hbm, out_sem.at[2]).wait()
    out_gg.wait()
    out_gu.wait()


def on_device(grad_out, gate_act, up_act, down_weight):
    bf, f32 = jnp.bfloat16, jnp.float32
    dma = pltpu.SemaphoreType.DMA
    hbm = pl.BlockSpec(memory_space=pl.ANY)
    return pl.pallas_call(
        kernel,
        out_shape=(
            jax.ShapeDtypeStruct((TB, FB), bf),
            jax.ShapeDtypeStruct((TB, FB), bf),
            jax.ShapeDtypeStruct((FB, DR), f32),
        ),
        in_specs=[hbm] * 4,
        out_specs=(hbm, hbm, hbm),
        scratch_shapes=[
            pltpu.VMEM((2, 4, TB, DR), bf),
            pltpu.VMEM((4, TB, DR), bf),
            pltpu.VMEM((2, FB, DR), bf),
            pltpu.VMEM((8, FB, TB), bf),
            pltpu.VMEM((3, TB, FB), bf),
            pltpu.VMEM((3, TB, FB), bf),
            pltpu.VMEM((TB, FB), f32),
            pltpu.VMEM((TB, FB), bf),
            pltpu.VMEM((TB, FB), bf),
            pltpu.VMEM((TB, FB), bf),
            pltpu.VMEM((TB, FB), bf),
            pltpu.VMEM((FB, DR), f32),
            dma((3,)), dma((3,)),
            dma((2,)), dma((8,)), dma((4,)), dma((4,)), dma((7,)), dma((8,)),
            dma((3,)), dma((3,)),
            dma((4,)), dma((4 * NQ,)), dma((4,)), dma((16,)),
            dma((2,)), dma((2 * NQ,)), dma((2,)), dma((8,)),
        ],
        compiler_params=pltpu.CompilerParams(
            collective_id=0, has_side_effects=True, vmem_limit_bytes=60 * 1024 * 1024
        ),
    )(grad_out, gate_act, up_act, down_weight)


def solution(mesh):
    placed = (P("row", "col"), P("row", "col"), P("row", "col"), P("col", "row"))
    return jax.shard_map(
        on_device,
        mesh=mesh,
        in_specs=placed,
        out_specs=(P("row", "col"), P("row", "col"), P("col", "row")),
        check_vma=False,
    )
```

time: 607 us -> 131 us (0.22)
  the two profiles are of different devices: /device:TPU:3 before, /device:TPU:14 now
where the time goes in v1:
time: 131 us
  Pallas kernels  122 us (93%)
  local copies, waits for them, and re-layouts  8.37 us (6%)
    pallas_call x1, Pallas kernels, on_device(): pl.pallas_call(kernel, out_shape=(jax.ShapeDtypeStruct((TB, FB), bf), jax...  122 us
    unnamed x3, local copies, waits for them, and re-layouts  8.37 us

profile of v1, /device:TPU:14, one launch (start us, length us, event | category | flops | bytes accessed | tf_op | source)
XLA Modules:
  0.0 130.8 jit_solution(874803834013277668)
XLA Ops:
  0.6 121.8 %shard_map.67 = (bf16[384,896]{1,0:T(8,128)(2,1)}, bf16[384,896]{1,0:T(8,128)(2,1)}, f32[896,1024]{1,0:T(8,128)}) custom-call(bf16[384,256]{1,0:T(8,128)(2,1)} %g_hbm.1, bf16[384,896]{1,0:T(8,128)(2,1)} %ga_hbm.1, bf16[384,896]{1,0:T(8,128)(2,1)} %up_hbm.1, bf16[896,1024]{1,0:T(8,128)(2,1)} %w_hbm.1), custom_call_target="tpu_custom_call" | custom-call | tf_op jit(solution)/shard_map/pallas_call | solution.py:334
  122.4 2.0 %copy.10 = bf16[384,896]{1,0:T(8,128)(2,1)} copy(bf16[384,896]{1,0:T(8,128)(2,1)} %get-tuple-element.6) | data formatting | bytes 1376256
  124.4 2.0 %copy.11 = bf16[384,896]{1,0:T(8,128)(2,1)} copy(bf16[384,896]{1,0:T(8,128)(2,1)} %get-tuple-element.7) | data formatting | bytes 1376256
  126.4 4.4 %copy.12 = f32[896,1024]{1,0:T(8,128)} copy(f32[896,1024]{1,0:T(8,128)} %get-tuple-element.8) | data formatting | bytes 7340032

commit v2 on v1

v2 whole, which is shorter than its diff:
```python
import functools

import jax
import jax.numpy as jnp
from jax import lax
from jax.experimental import pallas as pl
from jax.experimental.pallas import tpu as pltpu
from jax.sharding import PartitionSpec as P

MESH = pl.DeviceIdType.MESH
TB = 384
FB = 896
DR = 1024
DC = 256
CH = 8
NQ = 4 * CH
AP = CH // 2
AROWS = TB // AP
ROWS = TB // CH
HOPS = 7
W_AT = (25, 33, 42, 48)
AT_PASS, AT_OWN, AT_PARTNER = 18, 24, 37
LATER = 3
SKEW = 3
F_TILES = ((0, 256), (256, 256), (512, 256), (768, 128))


ORDER = ((0, 0), (0, 1), (2, 0), (2, 1), (1, 0), (3, 0), (1, 1), (3, 1))
HALF = TB // 2
FIRST = 2
HQ = CH // 2


def offset_of(h):
    return jnp.where(h < 2, 0, jnp.where(h < 4, 2, 1 + 2 * lax.rem(h, 2)))


def half_of(h):
    m = lax.div(h, 2)
    return jnp.where(m < 2, lax.rem(h, 2), m - 2)


UP = (0, 384)
DOWN = (384, 512)


def kernel(
    g_hbm, ga_hbm, up_hbm, w_hbm, ggv, guv, gwv,
    g1, g2, w2, ht, part, got, acc, ga, up,
    loc_sem,
    send_a, recv_a, send_w, recv_w, send_h, recv_h, recv_u, recv_d,
    send_r, recv_r,
    send_z, recv_z, send_s, recv_s, send_o, recv_o, send_p, recv_p,
):
    r = lax.axis_index("row")
    c = lax.axis_index("col")
    y, xl = lax.div(r, 2), lax.rem(r, 2)
    z = lax.div(c, 4)
    xh = lax.rem(lax.div(c, 2), 2)
    k = lax.rem(c, 2)
    sib = (r, c + 1 - 2 * k)
    partner = (r + 1 - 2 * xl, c)
    outer = (r + 1 - 2 * xl, c + 2 - 4 * xh)
    c2 = c + 2 - 4 * xh

    def ring_y(o):
        return lax.rem(r + 2 * o, 8)

    z_next = (
        (r, lax.rem(c + 4, 32)),
        (r, lax.rem(c + 28, 32)),
    )

    def remote(src, dst, ssem, rsem, dev):
        return pltpu.make_async_remote_copy(
            src_ref=src, dst_ref=dst, send_sem=ssem, recv_sem=rsem,
            device_id=dev, device_id_type=MESH,
        )

    def arrived(ref, sem):
        pltpu.make_async_copy(ref, ref, sem).wait()

    load_ga = pltpu.make_async_copy(ga_hbm, ga, loc_sem.at[0])
    load_up = pltpu.make_async_copy(up_hbm, up, loc_sem.at[1])
    load_w = pltpu.make_async_copy(w_hbm, w2.at[xl], loc_sem.at[2])
    load_ga.start()
    load_up.start()
    load_w.start()

    barrier = pltpu.get_barrier_semaphore()
    peers = [(ring_y(o), c) for o in (1, 2, 3)]
    peers += [(ring_y(o), c2) for o in (0, 1, 2, 3)]
    peers += [sib, partner, outer, z_next[0], z_next[1]]
    for dev in peers:
        pl.semaphore_signal(barrier, inc=1, device_id=dev, device_id_type=MESH)

    pl.semaphore_wait(barrier, len(peers))

    yr = lax.div(z, 2)
    zb_own = lax.rem(z, 2)
    unit_cols = pl.ds(pl.multiple_of((2 * xh + k) * DC, DC), DC)
    root_row = 2 * yr + xl
    for p in range(AP):
        rows = pl.ds(p * AROWS, AROWS)
        src, dst = g_hbm.at[rows, :], g1.at[zb_own, y, rows, unit_cols]
        rsem = recv_a.at[(y * 2 + xh) * AP + p]
        remote(src, dst, send_a.at[1], rsem, (root_row, c2)).start()

        @pl.when(yr == y)
        def _(src=src, dst=dst, rsem=rsem):
            pltpu.make_async_copy(src, dst, rsem).start()

        @pl.when(yr != y)
        def _(src=src, dst=dst, rsem=rsem):
            remote(src, dst, send_a.at[0], rsem, (root_row, c)).start()

    load_ga.wait()
    load_up.wait()

    def hidden_tile(i, carry):
        cols = pl.ds(pl.multiple_of(i * 128, 128), 128)
        gv = ga[:, cols].astype(jnp.float32)
        uv = up[:, cols].astype(jnp.float32)
        hv = gv * jax.nn.sigmoid(gv) * uv
        ht[r, cols, :] = hv.T.astype(jnp.bfloat16)
        return carry

    lax.fori_loop(0, FB // 128, hidden_tile, 0)

    h_sends = []

    def send_hidden(slot, rows, rsem, dev):
        ref = ht.at[slot, pl.ds(*rows), :]
        d = remote(ref, ref, send_h.at[len(h_sends)], rsem, dev)
        h_sends.append(d)
        d.start()

    y_up, y_down, y_far = [(ring_y(o), c) for o in (1, 3, 2)]

    def to_neighbours(slot):
        for dev in (y_up, y_down):
            send_hidden(slot, (0, FB), recv_h.at[slot], dev)

    def relay_hidden(kind, base):
        below, above = lax.rem(base + 6, 8), lax.rem(base + 2, 8)
        arrived(ht.at[below], recv_h.at[below])
        send_hidden(below, UP, recv_u.at[kind], y_up)
        arrived(ht.at[above], recv_h.at[above])
        send_hidden(above, DOWN, recv_d.at[kind], y_down)

    to_neighbours(r)
    send_hidden(r, (0, FB), recv_h.at[r], partner)

    w_sends = []
    for i, (f0, fn) in enumerate(F_TILES):
        w_sends.append(
            remote(
                w_hbm.at[pl.ds(f0, fn), :], w2.at[xl, pl.ds(f0, fn), :],
                send_w.at[i], recv_w.at[i], partner,
            )
        )
        w_sends[-1].start()

    def lane_distance(zb, way):
        root = 2 * y + zb
        if way == 0:
            return lax.rem(z - root + 8, 8)
        return lax.rem(root - z + 8, 8)

    def lane_cols(way):
        return pl.ds(pl.multiple_of((2 * way + k) * DC, DC), DC)

    def piece_of(q):
        h = lax.div(q, HQ)
        p = half_of(h) * HQ + lax.rem(q, HQ)
        rows = pl.ds(pl.multiple_of(p * ROWS, ROWS), ROWS)
        return h, lax.rem(y + offset_of(h), 4), p, rows

    def z_step(s, carry):
        for zb in range(2):
            for way in range(2):
                lane = 2 * zb + way
                d = lane_distance(zb, way)
                q = s - SKEW * d

                @pl.when(jnp.logical_and(q >= 0, q < NQ))
                def _(zb=zb, way=way, lane=lane, d=d, q=q):
                    h, yb, p, rows = piece_of(q)
                    ref = g1.at[zb, yb, rows, lane_cols(way)]

                    @pl.when(jnp.logical_and(d == 0, lax.rem(p, 2) == 0))
                    def _():
                        m = lax.div(p, 2)
                        piece = pl.ds(pl.multiple_of(m * AROWS, AROWS), AROWS)
                        arrived(
                            g1.at[zb, yb, piece, lane_cols(way)],
                            recv_a.at[(yb * 2 + way) * AP + m],
                        )

                    @pl.when(d != 0)
                    def _():
                        arrived(ref, recv_z.at[lane * NQ + q])

                    @pl.when(d < HOPS)
                    def _():
                        remote(
                            ref, ref, send_z.at[lane], recv_z.at[lane * NQ + q], z_next[way]
                        ).start()

                    remote(ref, ref, send_s.at[lane], recv_s.at[lane * 8 + h], sib).start()

                    @pl.when(xl == 1 - zb)
                    def _():
                        remote(
                            ref, g2.at[yb, rows, lane_cols(way)],
                            send_o.at[way], recv_o.at[way * NQ + q], outer,
                        ).start()

        for way in range(2):
            d = jnp.where(xl == 0, lane_distance(0, way), lane_distance(1, way))
            q = s - LATER - SKEW * d

            @pl.when(jnp.logical_and(q >= 0, q < NQ))
            def _(way=way, q=q):
                h, yb, p, rows = piece_of(q)
                ref = g2.at[yb, rows, lane_cols(way)]
                arrived(ref, recv_o.at[way * NQ + q])
                remote(ref, ref, send_p.at[way], recv_p.at[way * 8 + h], sib).start()

        return carry

    slot_p = r + 1 - 2 * xl
    nt = (((1,), (1,)), ((), ()))

    def product(yb, half, f0, fn):
        total = None
        for zb in range(2):
            term = lax.dot_general(
                g1[zb, yb, half * HALF : (half + 1) * HALF, :], w2[zb, pl.ds(f0, fn), :], nt,
                preferred_element_type=jnp.float32,
            )
            total = term if total is None else total + term
        return total

    def half_ready(h):
        o, half = ORDER[h]
        yb = lax.rem(y + o, 4)
        for zb in range(2):
            for way in range(2):
                lane = 2 * zb + way
                cols = pl.ds(pl.multiple_of((2 * way + 1 - k) * DC, DC), DC)
                ref = g1.at[zb, yb, pl.ds(half * HALF, HALF), cols]
                arrived(ref, recv_s.at[lane * 8 + h])

    def cell(h, t):
        o, half = ORDER[h]
        f0, fn = F_TILES[t]
        if t == 0:
            half_ready(h)
        if h == FIRST:
            arrived(w2.at[1 - xl, pl.ds(f0, fn), :], recv_w.at[t])
        rows = pl.ds(half * HALF, HALF)
        tile = product(lax.rem(y + o, 4), half, f0, fn)
        part[o - 1, half * HALF : (half + 1) * HALF, f0 : f0 + fn] = tile.astype(jnp.bfloat16)
        src = part.at[o - 1, rows, pl.ds(f0, fn)]
        dst = got.at[o - 1, rows, pl.ds(f0, fn)]
        rsem = recv_r.at[(2 * (o - 1) + half) * 4 + t]
        remote(src, dst, send_r.at[o - 1], rsem, (ring_y(o), c)).start()

    def pass_on():
        arrived(ht.at[slot_p], recv_h.at[slot_p])
        to_neighbours(slot_p)

    def opposite_hidden(kind, base):
        slot = lax.rem(base + 4, 8)
        arrived(ht.at[slot, pl.ds(*UP), :], recv_u.at[kind])
        arrived(ht.at[slot, pl.ds(*DOWN), :], recv_d.at[kind])

    def extra_ready(o):
        yb = lax.rem(y + o, 4)
        for h in range(8):
            if ORDER[h][0] == o:
                for way in range(2):
                    cols = pl.ds(pl.multiple_of((2 * way + 1 - k) * DC, DC), DC)
                    ref = g2.at[yb, pl.ds(ORDER[h][1] * HALF, HALF), cols]
                    arrived(ref, recv_p.at[way * 8 + h])

    def weight_pass(blocks, first=False, last=False):
        def tile(i, carry):
            cols = pl.ds(pl.multiple_of(i * 256, 256), 256)
            total = None if first else gwv[:, cols]
            for kind, o in blocks:
                yb = lax.rem(y + o, 4)
                left = ht[2 * yb + (xl if kind == 0 else 1 - xl)]
                right = g1[xl, yb, :, cols] if kind == 0 else g2[yb, :, cols]
                term = jnp.dot(left, right, preferred_element_type=jnp.float32)
                total = term if total is None else total + term
            gwv[:, cols] = total
            return carry

        lax.fori_loop(0, DR // 256, tile, 0)

    def own_weights():
        half_ready(0)
        half_ready(1)
        weight_pass([(0, 0)], first=True)

    def opposite_weights():
        opposite_hidden(0, r)
        weight_pass([(0, 2)])

    def extra_weights():
        extra_ready(0)
        weight_pass([(1, 0)])

    base = SKEW * HOPS
    ready = [base + HQ * (h + 1) for h in range(8)]
    events = [
        (AT_PASS, pass_on),
        (AT_OWN, lambda: relay_hidden(0, r)),
        (AT_PARTNER, lambda: relay_hidden(1, slot_p)),
        (ready[1] + 2, own_weights),
        (ready[2] + 3, extra_weights),
        (ready[4] + 3, opposite_weights),
    ]
    for h in range(FIRST, 8):
        for t in range(4):
            step = max(ready[h] + 1 + t // 2, W_AT[t])
            events.append((step, functools.partial(cell, h, t)))
    events.append((NQ + base + LATER, lambda: None))
    load_w.wait()
    at = 0
    for step, event in sorted(events, key=lambda e: e[0]):
        if step > at:
            lax.fori_loop(at, step, z_step, 0)
        event()
        at = step

    for half in range(2):
        for f0, fn in F_TILES:
            acc[half * HALF : (half + 1) * HALF, f0 : f0 + fn] = product(y, half, f0, fn)
    for o in range(1, 4):
        extra_ready(o)
    opposite_hidden(1, slot_p)
    weight_pass([(0, 1), (0, 3), (1, 1), (1, 2), (1, 3)], last=True)

    for i in range(3):
        for half in range(2):
            for t, (f0, fn) in enumerate(F_TILES):
                ref = got.at[i, pl.ds(half * HALF, HALF), pl.ds(f0, fn)]
                arrived(ref, recv_r.at[(2 * i + half) * 4 + t])

    def final_tile(i, carry):
        rows = pl.ds(pl.multiple_of(i * 32, 32), 32)
        gv = ga[rows, :].astype(jnp.float32)
        uv = up[rows, :].astype(jnp.float32)
        gh = acc[rows, :]
        for n in range(3):
            gh = gh + got[n, rows, :].astype(jnp.float32)
        s = jax.nn.sigmoid(gv)
        ggv[rows, :] = (gh * uv * s * (1.0 + gv * (1.0 - s))).astype(jnp.bfloat16)
        guv[rows, :] = (gh * (gv * s)).astype(jnp.bfloat16)
        return carry

    lax.fori_loop(0, TB // 32, final_tile, 0)
    @pl.when(yr != y)
    def _():
        arrived(g_hbm, send_a.at[0])

    arrived(g_hbm, send_a.at[1])
    for d in h_sends + w_sends:
        d.wait_send()
    for i in range(3):
        arrived(part.at[i], send_r.at[i])
    for zb in range(2):
        for way in range(2):
            lane = 2 * zb + way
            whole = g1.at[zb, :, :, lane_cols(way)]

            @pl.when(lane_distance(zb, way) < HOPS)
            def _(whole=whole, lane=lane):
                arrived(whole, send_z.at[lane])

            arrived(whole, send_s.at[lane])
    for way in range(2):
        whole = g2.at[:, :, lane_cols(way)]
        arrived(whole, send_o.at[way])
        arrived(whole, send_p.at[way])


def on_device(grad_out, gate_act, up_act, down_weight):
    bf, f32 = jnp.bfloat16, jnp.float32
    dma = pltpu.SemaphoreType.DMA
    hbm = pl.BlockSpec(memory_space=pl.ANY)
    return pl.pallas_call(
        kernel,
        out_shape=(
            pltpu.VMEM((TB, FB), bf),
            pltpu.VMEM((TB, FB), bf),
            pltpu.VMEM((FB, DR), f32),
        ),
        in_specs=[hbm] * 4,
        out_specs=(pl.BlockSpec(memory_space=pltpu.VMEM),) * 3,
        scratch_shapes=[
            pltpu.VMEM((2, 4, TB, DR), bf),
            pltpu.VMEM((4, TB, DR), bf),
            pltpu.VMEM((2, FB, DR), bf),
            pltpu.VMEM((8, FB, TB), bf),
            pltpu.VMEM((3, TB, FB), bf),
            pltpu.VMEM((3, TB, FB), bf),
            pltpu.VMEM((TB, FB), f32),
            pltpu.VMEM((TB, FB), bf),
            pltpu.VMEM((TB, FB), bf),
            dma((3,)),
            dma((2,)), dma((8 * AP,)), dma((4,)), dma((4,)), dma((9,)), dma((8,)), dma((2,)), dma((2,)),
            dma((3,)), dma((24,)),
            dma((4,)), dma((4 * NQ,)), dma((4,)), dma((32,)),
            dma((2,)), dma((2 * NQ,)), dma((2,)), dma((16,)),
        ],
        compiler_params=pltpu.CompilerParams(
            collective_id=0, has_side_effects=True, vmem_limit_bytes=46 * 1024 * 1024
        ),
    )(grad_out, gate_act, up_act, down_weight)


def solution(mesh):
    placed = (P("row", "col"), P("row", "col"), P("row", "col"), P("col", "row"))
    return jax.shard_map(
        on_device,
        mesh=mesh,
        in_specs=placed,
        out_specs=(P("row", "col"), P("row", "col"), P("col", "row")),
        check_vma=False,
    )
```

time: 131 us -> 111 us (0.85)
  the two profiles are of different devices: /device:TPU:14 before, /device:TPU:3 now
where the time goes in v2:
time: 111 us; the launch traced here: 110 us
  Pallas kernels  102 us (92%)
  local copies, waits for them, and re-layouts  6.65 us (6%)
    pallas_call x1, Pallas kernels, on_device(): pl.pallas_call(kernel, out_shape=(pltpu.VMEM((TB, FB), bf), pltpu.VMEM((T...  102 us
    unnamed x9, local copies, waits for them, and re-layouts  6.65 us

profile of v2, /device:TPU:3, one launch (start us, length us, event | category | flops | bytes accessed | tf_op | source)
XLA Modules:
  0.0 109.7 jit_solution(13256071786041392400)
XLA Ops:
  0.6 0.0 copy-start
  0.6 1.1 copy-done
  1.7 0.0 copy-start.1
  1.7 1.1 copy-done.1
  2.8 0.0 copy-start.2
  2.8 0.9 copy-done.2
  3.8 102.4 %shard_map.67 = (bf16[384,896]{1,0:T(8,128)(2,1)S(1)}, bf16[384,896]{1,0:T(8,128)(2,1)S(1)}, f32[896,1024]{1,0:T(8,128)S(1)}) custom-call(bf16[384,256]{1,0:T(8,128)(2,1)S(1)} %copy-done.2, bf16[384,896]{1,0:T(8,128)(2,1)S(1)} %copy-done, bf16[384,896]{1,0:T(8,128)(2,1)S(1)} %copy-done.1, bf16[896,1024]{1,0:T(8,128)(2,1)} %w_hbm.1), custom_call_target="tpu_custom_call" | custom-call | tf_op jit(solution)/shard_map/pallas_call | solution.py:395
  106.2 0.8 copy.10
  107.1 0.8 copy.11
  107.9 1.8 %copy.12 = f32[896,1024]{1,0:T(8,128)} copy(f32[896,1024]{1,0:T(8,128)S(1)} %get-tuple-element.5) | data formatting | bytes 7340032
Async XLA Ops:
  0.6 1.1 %copy-start = (bf16[384,896]{1,0:T(8,128)(2,1)S(1)}, bf16[384,896]{1,0:T(8,128)(2,1)}, u32[]{:S(2)}) copy-start(bf16[384,896]{1,0:T(8,128)(2,1)} %ga_hbm.1) | copy-start | bytes 2064388
  1.7 1.1 %copy-start.1 = (bf16[384,896]{1,0:T(8,128)(2,1)S(1)}, bf16[384,896]{1,0:T(8,128)(2,1)}, u32[]{:S(2)}) copy-start(bf16[384,896]{1,0:T(8,128)(2,1)} %up_hbm.1) | copy-start | bytes 2064388
  2.8 0.9 copy-start.2

commit v3 on v2

--- a/solution.py
+++ b/solution.py
@@ -42,13 +42,16 @@
 
 UP = (0, 384)
 DOWN = (384, 512)
+OVER_Y = 512
+UP2, DOWN2 = (0, 256), (256, 256)
+OVER_X = (OVER_Y, FB - OVER_Y)
 
 
 def kernel(
     g_hbm, ga_hbm, up_hbm, w_hbm, ggv, guv, gwv,
     g1, g2, w2, ht, part, got, acc, ga, up,
     loc_sem,
-    send_a, recv_a, send_w, recv_w, send_h, recv_h, recv_u, recv_d,
+    send_a, recv_a, send_w, recv_w, send_h, recv_h, recv_u, recv_d, recv_x,
     send_r, recv_r,
     send_z, recv_z, send_s, recv_s, send_o, recv_o, send_p, recv_p,
 ):
@@ -94,6 +97,19 @@
     for dev in peers:
         pl.semaphore_signal(barrier, inc=1, device_id=dev, device_id_type=MESH)
 
+    load_ga.wait()
+    load_up.wait()
+
+    def hidden_tile(i, carry):
+        cols = pl.ds(pl.multiple_of(i * 128, 128), 128)
+        gv = ga[:, cols].astype(jnp.float32)
+        uv = up[:, cols].astype(jnp.float32)
+        hv = gv * jax.nn.sigmoid(gv) * uv
+        ht[r, cols, :] = hv.T.astype(jnp.bfloat16)
+        return carry
+
+    lax.fori_loop(0, FB // 128, hidden_tile, 0)
+
     pl.semaphore_wait(barrier, len(peers))
 
     yr = lax.div(z, 2)
@@ -114,19 +130,6 @@
         def _(src=src, dst=dst, rsem=rsem):
             remote(src, dst, send_a.at[0], rsem, (root_row, c)).start()
 
-    load_ga.wait()
-    load_up.wait()
-
-    def hidden_tile(i, carry):
-        cols = pl.ds(pl.multiple_of(i * 128, 128), 128)
-        gv = ga[:, cols].astype(jnp.float32)
-        uv = up[:, cols].astype(jnp.float32)
-        hv = gv * jax.nn.sigmoid(gv) * uv
-        ht[r, cols, :] = hv.T.astype(jnp.bfloat16)
-        return carry
-
-    lax.fori_loop(0, FB // 128, hidden_tile, 0)
-
     h_sends = []
 
     def send_hidden(slot, rows, rsem, dev):
@@ -137,18 +140,25 @@
 
     y_up, y_down, y_far = [(ring_y(o), c) for o in (1, 3, 2)]
 
-    def to_neighbours(slot):
+    def to_neighbours(slot, rows):
         for dev in (y_up, y_down):
-            send_hidden(slot, (0, FB), recv_h.at[slot], dev)
+            send_hidden(slot, rows, recv_h.at[slot], dev)
+
+    def over_x(slot, i):
+        send_hidden(slot, OVER_X, recv_x.at[i], partner)
 
     def relay_hidden(kind, base):
         below, above = lax.rem(base + 6, 8), lax.rem(base + 2, 8)
-        arrived(ht.at[below], recv_h.at[below])
-        send_hidden(below, UP, recv_u.at[kind], y_up)
-        arrived(ht.at[above], recv_h.at[above])
-        send_hidden(above, DOWN, recv_d.at[kind], y_down)
-
-    to_neighbours(r)
+        rows = pl.ds(0, (FB, OVER_Y)[kind])
+        arrived(ht.at[below, rows, :], recv_h.at[below])
+        send_hidden(below, (UP, UP2)[kind], recv_u.at[kind], y_up)
+        arrived(ht.at[above, rows, :], recv_h.at[above])
+        send_hidden(above, (DOWN, DOWN2)[kind], recv_d.at[kind], y_down)
+        if kind == 0:
+            over_x(below, 0)
+            over_x(above, 1)
+
+    to_neighbours(r, (0, FB))
     send_hidden(r, (0, FB), recv_h.at[r], partner)
 
     w_sends = []
@@ -269,12 +279,14 @@
 
     def pass_on():
         arrived(ht.at[slot_p], recv_h.at[slot_p])
-        to_neighbours(slot_p)
+        to_neighbours(slot_p, (0, OVER_Y))
 
     def opposite_hidden(kind, base):
         slot = lax.rem(base + 4, 8)
-        arrived(ht.at[slot, pl.ds(*UP), :], recv_u.at[kind])
-        arrived(ht.at[slot, pl.ds(*DOWN), :], recv_d.at[kind])
+        arrived(ht.at[slot, pl.ds(*(UP, UP2)[kind]), :], recv_u.at[kind])
+        arrived(ht.at[slot, pl.ds(*(DOWN, DOWN2)[kind]), :], recv_d.at[kind])
+        if kind == 0:
+            over_x(slot, 2)
 
     def extra_ready(o):
         yb = lax.rem(y + o, 4)
@@ -342,6 +354,9 @@
     for o in range(1, 4):
         extra_ready(o)
     opposite_hidden(1, slot_p)
+    for i, o in enumerate((3, 1, 2)):
+        slot = lax.rem(slot_p + 2 * o, 8)
+        arrived(ht.at[slot, pl.ds(*OVER_X), :], recv_x.at[i])
     weight_pass([(0, 1), (0, 3), (1, 1), (1, 2), (1, 3)], last=True)
 
     for i in range(3):
@@ -391,7 +406,7 @@
 def on_device(grad_out, gate_act, up_act, down_weight):
     bf, f32 = jnp.bfloat16, jnp.float32
     dma = pltpu.SemaphoreType.DMA
-    hbm = pl.BlockSpec(memory_space=pl.ANY)
+    hbm = pl.BlockSpec(memory_space=pltpu.HBM)
     return pl.pallas_call(
         kernel,
         out_shape=(
@@ -412,13 +427,13 @@
             pltpu.VMEM((TB, FB), bf),
             pltpu.VMEM((TB, FB), bf),
             dma((3,)),
-            dma((2,)), dma((8 * AP,)), dma((4,)), dma((4,)), dma((9,)), dma((8,)), dma((2,)), dma((2,)),
+            dma((2,)), dma((8 * AP,)), dma((4,)), dma((4,)), dma((12,)), dma((8,)), dma((2,)), dma((2,)), dma((3,)),
             dma((3,)), dma((24,)),
             dma((4,)), dma((4 * NQ,)), dma((4,)), dma((32,)),
             dma((2,)), dma((2 * NQ,)), dma((2,)), dma((16,)),
         ],
         compiler_params=pltpu.CompilerParams(
-            collective_id=0, has_side_effects=True, vmem_limit_bytes=46 * 1024 * 1024
+            collective_id=0, has_side_effects=True, vmem_limit_bytes=59 * 1024 * 1024
         ),
     )(grad_out, gate_act, up_act, down_weight)
 

time: 111 us -> 102 us (0.919); the launches traced: 110 us -> 102 us
  Pallas kernels: 102 us -> 97.9 us
  local copies, waits for them, and re-layouts: 6.65 us -> 3.53 us
    pallas_call x1, Pallas kernels: 102 us -> 97.9 us  [on_device(): pl.pallas_call(kernel, out_shape=(pltpu.VMEM((TB, FB), bf), pltpu.VMEM((T...]
    unnamed x9 -> x3, local copies, waits for them, and re-layouts: 6.65 us -> 3.53 us
where the time goes in v3:
time: 102 us
  Pallas kernels  97.9 us (96%)
  local copies, waits for them, and re-layouts  3.53 us (3%)
    pallas_call x1, Pallas kernels, on_device(): pl.pallas_call(kernel, out_shape=(pltpu.VMEM((TB, FB), bf), pltpu.VMEM((T...  97.9 us
    unnamed x3, local copies, waits for them, and re-layouts  3.53 us

profile of v3, /device:TPU:3, one launch (start us, length us, event | category | flops | bytes accessed | tf_op | source)
XLA Modules:
  0.0 102.1 jit_solution(14053226780835145275)
XLA Ops:
  0.6 97.9 %shard_map.67 = (bf16[384,896]{1,0:T(8,128)(2,1)S(1)}, bf16[384,896]{1,0:T(8,128)(2,1)S(1)}, f32[896,1024]{1,0:T(8,128)S(1)}) custom-call(bf16[384,256]{1,0:T(8,128)(2,1)} %g_hbm.1, bf16[384,896]{1,0:T(8,128)(2,1)} %ga_hbm.1, bf16[384,896]{1,0:T(8,128)(2,1)} %up_hbm.1, bf16[896,1024]{1,0:T(8,128)(2,1)} %w_hbm.1), custom_call_target="tpu_custom_call" | custom-call | tf_op jit(solution)/shard_map/pallas_call | solution.py:410
  98.5 0.8 copy.10
  99.4 0.8 copy.11
  100.2 1.8 %copy.12 = f32[896,1024]{1,0:T(8,128)} copy(f32[896,1024]{1,0:T(8,128)S(1)} %get-tuple-element.5) | data formatting | bytes 7340032

commit v4 on v3

--- a/solution.py
+++ b/solution.py
@@ -97,19 +97,6 @@
     for dev in peers:
         pl.semaphore_signal(barrier, inc=1, device_id=dev, device_id_type=MESH)
 
-    load_ga.wait()
-    load_up.wait()
-
-    def hidden_tile(i, carry):
-        cols = pl.ds(pl.multiple_of(i * 128, 128), 128)
-        gv = ga[:, cols].astype(jnp.float32)
-        uv = up[:, cols].astype(jnp.float32)
-        hv = gv * jax.nn.sigmoid(gv) * uv
-        ht[r, cols, :] = hv.T.astype(jnp.bfloat16)
-        return carry
-
-    lax.fori_loop(0, FB // 128, hidden_tile, 0)
-
     pl.semaphore_wait(barrier, len(peers))
 
     yr = lax.div(z, 2)
@@ -129,6 +116,19 @@
         @pl.when(yr != y)
         def _(src=src, dst=dst, rsem=rsem):
             remote(src, dst, send_a.at[0], rsem, (root_row, c)).start()
+
+    load_ga.wait()
+    load_up.wait()
+
+    def hidden_tile(i, carry):
+        cols = pl.ds(pl.multiple_of(i * 128, 128), 128)
+        gv = ga[:, cols].astype(jnp.float32)
+        uv = up[:, cols].astype(jnp.float32)
+        hv = gv * jax.nn.sigmoid(gv) * uv
+        ht[r, cols, :] = hv.T.astype(jnp.bfloat16)
+        return carry
+
+    lax.fori_loop(0, FB // 128, hidden_tile, 0)
 
     h_sends = []
 

time: 102 us -> 102 us (level)
  no operation moved by 1% of the time
where the time goes in v4:
time: 102 us
  Pallas kernels  97.9 us (96%)
  local copies, waits for them, and re-layouts  3.53 us (3%)
    pallas_call x1, Pallas kernels, on_device(): pl.pallas_call(kernel, out_shape=(pltpu.VMEM((TB, FB), bf), pltpu.VMEM((T...  97.9 us
    unnamed x3, local copies, waits for them, and re-layouts  3.53 us

profile of v4, /device:TPU:3, one launch (start us, length us, event | category | flops | bytes accessed | tf_op | source)
XLA Modules:
  0.0 102.1 jit_solution(8992153569205012084)
XLA Ops:
  0.6 97.9 %shard_map.67 = (bf16[384,896]{1,0:T(8,128)(2,1)S(1)}, bf16[384,896]{1,0:T(8,128)(2,1)S(1)}, f32[896,1024]{1,0:T(8,128)S(1)}) custom-call(bf16[384,256]{1,0:T(8,128)(2,1)} %g_hbm.1, bf16[384,896]{1,0:T(8,128)(2,1)} %ga_hbm.1, bf16[384,896]{1,0:T(8,128)(2,1)} %up_hbm.1, bf16[896,1024]{1,0:T(8,128)(2,1)} %w_hbm.1), custom_call_target="tpu_custom_call" | custom-call | tf_op jit(solution)/shard_map/pallas_call | solution.py:410
  98.5 0.8 copy.10
  99.4 0.8 copy.11
  100.2 1.8 %copy.12 = f32[896,1024]{1,0:T(8,128)} copy(f32[896,1024]{1,0:T(8,128)S(1)} %get-tuple-element.5) | data formatting | bytes 7340032
